TPU v7x, 32 devices: a whole 2x2x4 slice. The times are simulated.
32 devices in a mesh: dp: 4 (over z), head: 8 (over y, x, core).
Axes of the slice: x: 2, y: 2, z: 4, core: 2. Of those that a mesh axis runs over, the one named last changes fastest.
Arguments:
- tokens: bfloat16 [6144, 1152], P('dp'), may hold values from -6 to 6
- seg_ids: int32 [4, 1536], P('dp'), may hold values from 0 to 2, as said below
- time_steps: int32 [12], P('dp'), may hold values from 0 to 999
- head_masks: int32 [12, 16], P('dp', 'head'), may hold values 0 or 1
- skip_masks: int32 [4, 1536], P('dp'), may hold values 0 or 1
- ada_weight: bfloat16 [1152, 6912], P(None, 'head'), may hold values from -0.1875 to 0.1875
- ada_bias: bfloat16 [6912], P('head'), may hold values from -3 to 3
- qkv_weight: bfloat16 [1152, 3, 1152], P(None, None, 'head'), may hold values from -0.1875 to 0.1875
- qv_bias: bfloat16 [2, 1152], P(None, 'head'), may hold values from -2 to 2
- proj_weight: bfloat16 [1152, 1152], P('head'), may hold values from -3 to 3
- proj_bias: bfloat16 [1152], replicated, may hold values from -2 to 2
- fc1_weight: bfloat16 [1152, 4608], P(None, 'head'), may hold values from -0.1875 to 0.1875
- fc1_bias: bfloat16 [4608], P('head'), may hold values from -2 to 2
- fc2_weight: bfloat16 [4608, 1152], P('head'), may hold values from -0.09375 to 0.09375
- fc2_bias: bfloat16 [1152], replicated, may hold values from -2 to 2
- out_cotangent: bfloat16 [6144, 1152], P('dp'), may hold values from -6 to 6
Outputs:
- layer_out: bfloat16 [6144, 1152], P(('dp', 'head'))
- input_grad: float32 [6144, 1152], P(('dp', 'head'))
- ada_weight_grad: float32 [1152, 6912], P(None, 'head')
- ada_bias_grad: float32 [6912], P('head')
- qkv_weight_grad: float32 [1152, 3, 1152], P(None, None, 'head')
- qv_bias_grad: float32 [2, 1152], P(None, 'head')
- proj_weight_grad: float32 [1152, 1152], P('head')
- proj_bias_grad: float32 [1152], replicated
- fc1_weight_grad: float32 [1152, 4608], P(None, 'head')
- fc1_bias_grad: float32 [4608], P('head')
- fc2_weight_grad: float32 [4608, 1152], P('head')
- fc2_bias_grad: float32 [1152], replicated
Inputs may be any that keep to these rules, and one draw needn't show every extreme that they name: `seg_ids`: each pack holds one image of 1024 tokens and two images of 256 tokens, each on neighbouring positions, in an order that the draw chooses for each pack; the image numbers 0, 1, 2 never fall along a pack.
All inputs are finite; a program needn't handle non-finite values. No bound on the sum of `head_masks` or of `skip_masks` on one device may be relied on, other than what follows from the above.
Results may differ from a plain program's by a relative error of at most 0.01255.
The roundings to bfloat16 on the way count: a program that leaves them out, or rounds other values in their place, can miss the bound.
Values may be sent and summed in bfloat16 or wider, within the bound.
A program may use at most 192 MiB of HBM per device.

v0:
```python
import math

import jax
import jax.numpy as jnp
from jax import lax
from jax.sharding import PartitionSpec as P

HEAD_DIM = 72


highest = lax.Precision.HIGHEST


def embed_steps(steps, model_width):
    half_width = model_width // 2
    freqs = jnp.exp(-math.log(10000.0) * jnp.arange(half_width, dtype=jnp.float32) / half_width)
    angles = steps.astype(jnp.float32)[:, None] * freqs[None, :]
    return jnp.concatenate([jnp.cos(angles), jnp.sin(angles)], axis=1)


def normalize(value):
    center = value - jnp.mean(value, axis=-1, keepdims=True)
    return center * lax.rsqrt(jnp.mean(center * center, axis=-1, keepdims=True) + 1e-06)


def norm_back(value, grad):
    return jax.vjp(normalize, value)[1](grad)[0]


def gelu_tanh(value):
    return jax.nn.gelu(value, approximate=True)


def per_token(select, table):
    return jnp.dot(select, table, precision=highest)


def item_sums(select, values):
    return jnp.einsum("sg,sd->gd", select, values, precision=highest)


def attend_forward(queries, key_rows, value_rows, segment, heads_here, score_scale, block_rows):
    length = queries.shape[0]
    q_heads = queries.reshape(length, heads_here, -1)
    k_heads = key_rows.reshape(length, heads_here, -1)
    v_heads = value_rows.reshape(length, heads_here, -1)

    def one_block(start):
        q_block = lax.dynamic_slice_in_dim(q_heads, start, block_rows, 0)
        seg_query = lax.dynamic_slice_in_dim(segment, start, block_rows, 0)
        scores = (
            jnp.einsum("qhe,khe->hqk", q_block, k_heads, preferred_element_type=jnp.float32)
            * score_scale
        )
        scores = jnp.where((seg_query[:, None] == segment[None, :])[None], scores, -1e30)
        row_peak = jnp.max(scores, axis=-1, keepdims=True)
        row_exp = jnp.exp(scores - row_peak)
        row_total = jnp.sum(row_exp, axis=-1, keepdims=True)
        prob_low = (row_exp / row_total).astype(jnp.bfloat16)
        out_block = jnp.einsum(
            "hqk,khe->qhe", prob_low, v_heads, preferred_element_type=jnp.float32
        )
        return (out_block.reshape(block_rows, -1), (row_peak + jnp.log(row_total))[..., 0])

    starts = jnp.arange(length // block_rows, dtype=jnp.int32) * block_rows
    out_blocks, log_totals = lax.map(one_block, starts)
    return (out_blocks.reshape(length, -1), log_totals)


def attend_backward(
    queries,
    key_rows,
    value_rows,
    grad_attn,
    segment,
    log_totals,
    heads_here,
    score_scale,
    block_rows,
):
    length = queries.shape[0]
    q_heads = queries.reshape(length, heads_here, -1)
    k_heads = key_rows.reshape(length, heads_here, -1)
    v_heads = value_rows.reshape(length, heads_here, -1)
    g_heads = grad_attn.reshape(length, heads_here, -1)

    def one_block(carry, inputs):
        start, lse_block = inputs
        grad_keys_acc, grad_values_acc = carry
        q_block = lax.dynamic_slice_in_dim(q_heads, start, block_rows, 0)
        g_block = lax.dynamic_slice_in_dim(g_heads, start, block_rows, 0)
        seg_query = lax.dynamic_slice_in_dim(segment, start, block_rows, 0)
        scores = (
            jnp.einsum("qhe,khe->hqk", q_block, k_heads, preferred_element_type=jnp.float32)
            * score_scale
        )
        scores = jnp.where((seg_query[:, None] == segment[None, :])[None], scores, -1e30)
        probs = jnp.exp(scores - lse_block[..., None])
        grad_probs = jnp.einsum(
            "qhe,khe->hqk", g_block, v_heads, preferred_element_type=jnp.float32
        )
        row_delta = jnp.sum(grad_probs * probs, axis=-1, keepdims=True)
        grad_scores = (probs * (grad_probs - row_delta)).astype(jnp.bfloat16)
        grad_query = (
            jnp.einsum("hqk,khe->qhe", grad_scores, k_heads, preferred_element_type=jnp.float32)
            * score_scale
        )
        grad_keys_acc = grad_keys_acc + jnp.einsum(
            "hqk,qhe->khe", grad_scores, q_block, preferred_element_type=jnp.float32
        )
        grad_values_acc = grad_values_acc + jnp.einsum(
            "hqk,qhe->khe", probs.astype(jnp.bfloat16), g_block, preferred_element_type=jnp.float32
        )
        return (
            (grad_keys_acc, grad_values_acc),
            grad_query.astype(jnp.bfloat16).reshape(block_rows, -1),
        )

    starts = jnp.arange(length // block_rows, dtype=jnp.int32) * block_rows
    zeros_acc = jnp.zeros(k_heads.shape, jnp.float32)
    (grad_keys_acc, grad_values_acc), grad_query = lax.scan(
        one_block, (zeros_acc, zeros_acc), (starts, log_totals)
    )
    grad_keys = (grad_keys_acc * score_scale).astype(jnp.bfloat16).reshape(length, -1)
    grad_values = grad_values_acc.astype(jnp.bfloat16).reshape(length, -1)
    return (grad_query.reshape(length, -1), grad_keys, grad_values)


def local(
    tokens,
    seg_ids,
    time_steps,
    head_masks,
    skip_masks,
    ada_weight,
    ada_bias,
    qkv_weight,
    qv_bias,
    proj_weight,
    proj_bias,
    fc1_weight,
    fc1_bias,
    fc2_weight,
    fc2_bias,
    out_cotangent,
):
    length, model_width = tokens.shape
    groups = time_steps.shape[0]
    heads_here = qkv_weight.shape[2] // HEAD_DIM
    score_scale = HEAD_DIM ** (-0.5)
    block_rows = min(512, length)
    share_rows = length // lax.axis_size("head")
    row_start = lax.axis_index("head") * share_rows
    segment = seg_ids[0]
    keep_tok = skip_masks[0].astype(jnp.float32)[:, None]
    select = (segment[:, None] == jnp.arange(groups, dtype=jnp.int32)[None, :]).astype(jnp.float32)

    def own_rows(value):
        return lax.dynamic_slice_in_dim(value, row_start, share_rows, 0)

    time_act = jax.nn.silu(embed_steps(time_steps, model_width)).astype(jnp.bfloat16)
    mod_part = jnp.dot(time_act, ada_weight, preferred_element_type=jnp.float32) + ada_bias.astype(
        jnp.float32
    )
    modulation = lax.all_gather(mod_part, "head", axis=1, tiled=True)
    shift_one, scale_one, gate_one, shift_two, scale_two, gate_two = [
        per_token(select, table_piece) for table_piece in jnp.split(modulation, 6, axis=1)
    ]
    x_full = tokens.astype(jnp.float32)
    norm_one = normalize(x_full)
    h_one = (norm_one * (1.0 + scale_one) + shift_one).astype(jnp.bfloat16)
    proj_three = jnp.einsum("sd,dcj->csj", h_one, qkv_weight, preferred_element_type=jnp.float32)
    qv_float = qv_bias.astype(jnp.float32)
    queries = (proj_three[0] + qv_float[0]).astype(jnp.bfloat16)
    key_rows = proj_three[1].astype(jnp.bfloat16)
    value_rows = (proj_three[2] + qv_float[1]).astype(jnp.bfloat16)
    attended, log_totals = attend_forward(
        queries, key_rows, value_rows, segment, heads_here, score_scale, block_rows
    )
    head_keep = jnp.repeat(per_token(select, head_masks.astype(jnp.float32)), HEAD_DIM, axis=1)
    attn_low = (attended * head_keep).astype(jnp.bfloat16)
    attn_part = jnp.dot(attn_low, proj_weight, preferred_element_type=jnp.float32)
    proj_b = proj_bias.astype(jnp.float32)
    fc1_b = fc1_bias.astype(jnp.float32)
    fc2_b = fc2_bias.astype(jnp.float32)
    branch_a = lax.psum(attn_part, "head") + proj_b
    mid_rows = x_full + gate_one * branch_a
    norm_two = normalize(mid_rows)
    h_two = (norm_two * (1.0 + scale_two) + shift_two).astype(jnp.bfloat16)
    hidden = jnp.dot(h_two, fc1_weight, preferred_element_type=jnp.float32) + fc1_b
    gelu_out = gelu_tanh(hidden).astype(jnp.bfloat16)
    mlp_part = jnp.dot(gelu_out, fc2_weight, preferred_element_type=jnp.float32)
    grad_y = out_cotangent.astype(jnp.float32)
    grad_m = (grad_y * gate_two * keep_tok).astype(jnp.bfloat16)
    branch_m = lax.psum(mlp_part.astype(jnp.bfloat16), "head").astype(jnp.float32) + fc2_b
    layer_full = mid_rows + gate_two * keep_tok * branch_m
    layer_out = own_rows(layer_full).astype(jnp.bfloat16)
    gate_two_grad = item_sums(select, grad_y * keep_tok * branch_m)
    fc2_grad = jnp.einsum("sf,sd->fd", gelu_out, grad_m, preferred_element_type=jnp.float32)
    fc2_bias_grad = jnp.sum(grad_m.astype(jnp.float32), axis=0)
    grad_gelu = jnp.einsum("sd,fd->sf", grad_m, fc2_weight, preferred_element_type=jnp.float32)
    grad_hidden = jax.vjp(gelu_tanh, hidden)[1](grad_gelu)[0].astype(jnp.bfloat16)
    fc1_grad = jnp.einsum("sd,sf->df", h_two, grad_hidden, preferred_element_type=jnp.float32)
    fc1_bias_grad = jnp.sum(grad_hidden.astype(jnp.float32), axis=0)
    h_two_part = jnp.einsum(
        "sf,df->sd", grad_hidden, fc1_weight, preferred_element_type=jnp.float32
    )
    grad_h_two = lax.psum(h_two_part, "head")
    grad_mid = grad_y + norm_back(mid_rows, grad_h_two * (1.0 + scale_two))
    shift_two_grad = item_sums(select, grad_h_two)
    scale_two_grad = item_sums(select, grad_h_two * norm_two)
    gate_one_grad = item_sums(select, grad_mid * branch_a)
    grad_a = (grad_mid * gate_one).astype(jnp.bfloat16)
    proj_bias_grad = jnp.sum(grad_a.astype(jnp.float32), axis=0)
    proj_grad = jnp.einsum("sj,sd->jd", attn_low, grad_a, preferred_element_type=jnp.float32)
    grad_attn_low = jnp.einsum(
        "sd,jd->sj", grad_a, proj_weight, preferred_element_type=jnp.float32
    ).astype(jnp.bfloat16)
    grad_attn = grad_attn_low * head_keep.astype(jnp.bfloat16)
    grad_queries, grad_keys, grad_values = attend_backward(
        queries,
        key_rows,
        value_rows,
        grad_attn,
        segment,
        log_totals,
        heads_here,
        score_scale,
        block_rows,
    )
    grad_three = jnp.stack([grad_queries, grad_keys, grad_values])
    qkv_grad = jnp.einsum("sd,csj->dcj", h_one, grad_three, preferred_element_type=jnp.float32)
    qv_bias_grad = jnp.stack(
        [
            jnp.sum(grad_queries.astype(jnp.float32), axis=0),
            jnp.sum(grad_values.astype(jnp.float32), axis=0),
        ]
    )
    h_one_part = jnp.einsum(
        "csj,dcj->sd", grad_three, qkv_weight, preferred_element_type=jnp.float32
    )
    grad_h_one = lax.psum(h_one_part, "head")
    grad_input = grad_mid + norm_back(x_full, grad_h_one * (1.0 + scale_one))
    input_grad = own_rows(grad_input)
    shift_one_grad = item_sums(select, grad_h_one)
    scale_one_grad = item_sums(select, grad_h_one * norm_one)
    mod_grad = jnp.concatenate(
        [
            shift_one_grad,
            scale_one_grad,
            gate_one_grad,
            shift_two_grad,
            scale_two_grad,
            gate_two_grad,
        ],
        axis=1,
    )
    col_count = ada_weight.shape[1]
    mod_cols = lax.dynamic_slice_in_dim(mod_grad, lax.axis_index("head") * col_count, col_count, 1)
    ada_grad = jnp.einsum("gd,gc->dc", time_act.astype(jnp.float32), mod_cols, precision=highest)
    ada_bias_grad = jnp.sum(mod_cols, axis=0)
    summed = lax.psum(
        (
            ada_grad,
            ada_bias_grad,
            qkv_grad,
            qv_bias_grad,
            proj_grad,
            proj_bias_grad,
            fc1_grad,
            fc1_bias_grad,
            fc2_grad,
            fc2_bias_grad,
        ),
        "dp",
    )
    return (layer_out, input_grad) + tuple(summed)


def solution(mesh):
    placed = (
        P("dp", None),
        P("dp", None),
        P("dp"),
        P("dp", "head"),
        P("dp", None),
        P(None, "head"),
        P("head"),
        P(None, None, "head"),
        P(None, "head"),
        P("head", None),
        P(),
        P(None, "head"),
        P("head"),
        P("head", None),
        P(),
        P("dp", None),
    )
    return jax.shard_map(
        local,
        mesh=mesh,
        in_specs=placed,
        out_specs=(
            P(("dp", "head"), None),
            P(("dp", "head"), None),
            P(None, "head"),
            P("head"),
            P(None, None, "head"),
            P(None, "head"),
            P("head", None),
            P(),
            P(None, "head"),
            P("head"),
            P("head", None),
            P(),
        ),
        check_vma=False,
    )
```

profile of v0, /device:TPU:29, one launch (start us, length us, event | category | flops | bytes accessed | tf_op | source)
XLA Modules:
  0.0 1049.6 jit_solution(16489668344534000772)
XLA Ops:
  17.1 9.7 all-gather
  40.2 43.0 %while.27 = (s32[]{:T(128)}, f32[3,512,144]{1,0,2:T(4,128)S(1)}, f32[3,2,512]{2,1,0:T(2,128)S(1)}, s32[3]{0:T(128)S(1)}, s32[1536]{0:T(1024)S(1)}, /*index=5*/s3...) while((s32[]{:T(128)}, f32[3,512,144]{1,0,2:T(4,128)S(1)}, ...), condition=%wide.region_5.6_spmd, body=%wide.region_2.5_spmd.sunk | while | flops 472644608 | bytes 24584384 | solution.py:66
  88.4 5.7 convolution_add_fusion.1
  94.1 6.8 convert_reduce_fusion.1
  107.1 92.8 %all-reduce.8.cloned.1.call-done = f32[1536,1152]{1,0:T(8,128)} async-done(((f32[1536,1152]{1,0:T(8,128)}), f32[1536,1152]{1,0:T(8,128)}) %all-reduce.8.cloned.1.call-update) | async-done | bytes 7077904 | tf_op jit(solution)/shard_map/psum | solution.py:186
  199.9 8.9 fusion.116
  209.7 8.8 fusion.34
  218.5 6.6 convert_reduce_fusion.3
  231.7 113.0 %all-reduce.12.cloned.1.call-done = f32[1536,1152]{1,0:T(8,128)} async-done(((f32[1536,1152]{1,0:T(8,128)}), f32[1536,1152]{1,0:T(8,128)}) %all-reduce.12.cloned.1.call-update) | async-done | bytes 7077904 | tf_op jit(solution)/shard_map/psum | solution.py:208
  344.7 8.1 multiply_reduce_fusion.1
  353.8 6.9 fusion.115
  369.3 46.7 %while.28 = (s32[]{:T(128)}, f32[1536,2,72]{0,2,1:T(8,128)S(1)}, f32[1536,2,72]{0,2,1:T(8,128)S(1)}, bf16[3,512,144]{1,2,0:T(8,128)(2,1)}, s32[3]{0:T(128)S(1)},...) while((s32[]{:T(128)}, f32[1536,2,72]{0,2,1:T(8,128)S(1)}, ...), condition=%wide.region_15.16_spmd.clone, body=%wide.region_13.15_spmd.clone.sunk | while | flops 1148435456 | bytes 54702316 | solution.py:121
  418.2 6.3 convolution_bitcast_fusion.1
  425.2 6.9 fusion.124
  436.9 7.8 fusion.111
  452.3 85.4 %all-reduce.14.cloned.1.call-done = f32[1536,1152]{1,0:T(8,128)} async-done(((f32[1536,1152]{1,0:T(8,128)}), f32[1536,1152]{1,0:T(8,128)}) %all-reduce.14.cloned.1.call-update) | async-done | bytes 7077904 | tf_op jit(solution)/shard_map/psum | solution.py:242
  543.3 5.6 fusion.68
  549.0 7.4 fusion.71
  562.4 52.6 %all-reduce.10.cloned.1.call-done = bf16[1536,1152]{1,0:T(8,128)(2,1)} async-done(((bf16[1536,1152]{1,0:T(8,128)(2,1)}), bf16[1536,1152]{1,0:T(8,128)(2,1)}) %all-reduce.10.cloned.1.call-update) | async-done | bytes 3538960 | tf_op jit(solution)/shard_map/psum | solution.py:195
  615.0 6.3 fusion.65
  630.4 8.3 fusion.38
  638.8 8.5 fusion.114
  647.5 19.6 %all-reduce = (f32[864]{0:T(1024)}, f32[2,144]{1,0:T(2,128)}, f32[1152]{0:T(1024)}, f32[576]{0:T(1024)}, f32[1152]{0:T(1024)}) all-reduce(f32[864]{0:T(1024)S(1)} %dynamic-slice_reduce_fusion, f32[2,144]{1,0:T(2,128)S(1)} %pad_maximum_fusion.2, f32[1152]{0:T(1024)S(1)} %copy-done.40, ...), channel_id=1, replica_groups=mesh['dp'=4,'head'=8] {'dp'}, use_global_device_ids=true, to_apply=%region_21.22 | all-reduce | flops 4032 | bytes 32256 | tf_op jit(solution)/shard_map/psum | solution.py:262
  669.6 363.4 %all-reduce.16.cloned.1.call-done = (f32[1152,864]{0,1:T(8,128)}, f32[1152,3,144]{0,2,1:T(8,128)}, f32[144,1152]{1,0:T(8,128)}, f32[1152,576]{0,1:T(8,128)}, f32[576,1152]{1,0:T(8,128)}) async-done(((f32[1152,864]{0,1:T(8,128)}, f32[1152,3,144]{0,2,1:T(8,128)}, f32[144,1152]{1,0:T(8,128)}, f32[1152,576]{0,1:T(8,128)}, f32[576,1152]{1,0:T(8,128)}), (f32[1152,864]{0,1:T(8,128)}, f32[1152,3,144]{0,2,1:T(8,128)}, ...) | async-done | bytes 11943952 | tf_op jit(solution)/shard_map/psum | solution.py:262
  (275 shorter events, 177.0 us)
Async XLA Ops:
  7.2 9.3 copy-start
  7.2 192.7 %all-reduce.8.cloned.1.call-start = ((), (), s32[]{:S(2)}) async-start(), calls=%async_computation | async-start | bytes 14155776 | tf_op jit(solution)/shard_map/psum | solution.py:186
  12.0 18.1 %copy-start.25 = (f32[1536]{0:T(1024)}, f32[1536]{0:T(1024)S(1)}, u32[]{:S(2)}) copy-start(f32[1536]{0:T(1024)S(1)} %broadcast_multiply_fusion.1) | copy-start | bytes 18436
  15.7 14.4 %copy-start.27 = (f32[1536]{0:T(1024)}, f32[1536]{0:T(1024)S(1)}, u32[]{:S(2)}) copy-start(f32[1536]{0:T(1024)S(1)} %fusion.105) | copy-start | bytes 18436
  40.2 43.4 %copy-start.23 = (bf16[144,1152]{1,0:T(8,128)(2,1)S(1)}, bf16[144,1152]{1,0:T(8,128)(2,1)}, u32[]{:S(2)}) copy-start(bf16[144,1152]{1,0:T(8,128)(2,1)} %param.29) | copy-start | bytes 995332
  87.7 257.0 %all-reduce.12.cloned.1.call-start = ((), (), s32[]{:S(2)}) async-start(), calls=%async_computation.2 | async-start | bytes 14155776 | tf_op jit(solution)/shard_map/psum | solution.py:208
  88.4 111.5 %copy-start.33 = (f32[1152]{0:T(1024)}, f32[1152]{0:T(1024)S(1)}, u32[]{:S(2)}) copy-start(f32[1152]{0:T(1024)S(1)} %convert_element_type.140) | copy-start | bytes 13828
  94.1 8.7 copy-start.48
  208.8 9.7 copy-start.2
  209.7 8.8 copy-start.47
  209.7 8.8 copy-start.53
  231.5 306.1 %all-reduce.14.cloned.1.call-start = ((), (), s32[]{:S(2)}) async-start(), calls=%async_computation.3 | async-start | bytes 14155776 | tf_op jit(solution)/shard_map/psum | solution.py:242
  344.7 9.1 copy-start.6
  344.7 16.0 %slice-start.4 = ((s8[7077888]{0:T(1024)(128)(4,1)}), s8[4194304]{0:T(1024)(128)(4,1)S(1)}, s32[]{:S(2)}) async-start(s8[7077888]{0:T(1024)(128)(4,1)} %bitcast.122), calls=%async_computation.9 | async-start | bytes 8388608
  424.5 190.4 %all-reduce.10.cloned.1.call-start = ((), (), s32[]{:S(2)}) async-start(), calls=%async_computation.1 | async-start | bytes 7077888 | tf_op jit(solution)/shard_map/psum | solution.py:195
  444.8 588.2 %all-reduce.16.cloned.1.call-start = ((), (), s32[]{:S(2)}) async-start(), calls=%async_computation.4 | async-start | bytes 23887872 | tf_op jit(solution)/shard_map/psum | solution.py:262
  449.1 94.2 %copy-start.26 = (f32[1536]{0:T(1024)S(1)}, f32[1536]{0:T(1024)}, u32[]{:S(2)}) copy-start(f32[1536]{0:T(1024)} %copy-done.25) | copy-start | bytes 18436
  449.1 94.2 %copy-start.28 = (f32[1536]{0:T(1024)S(1)}, f32[1536]{0:T(1024)}, u32[]{:S(2)}) copy-start(f32[1536]{0:T(1024)} %copy-done.27) | copy-start | bytes 18436
  543.3 13.1 %slice-start.2 = ((s8[7077888]{0:T(1024)(128)(4,1)}), s8[4194304]{0:T(1024)(128)(4,1)S(1)}, s32[]{:S(2)}) async-start(s8[7077888]{0:T(1024)(128)(4,1)} %bitcast.120), calls=%async_computation.7 | async-start | bytes 8388608
  543.3 15.6 %slice-start = ((s8[7077888]{0:T(1024)(128)(4,1)}), s8[4194304]{0:T(1024)(128)(4,1)S(1)}, s32[]{:S(2)}) async-start(s8[7077888]{0:T(1024)(128)(4,1)} %bitcast.118), calls=%async_computation.5 | async-start | bytes 8388608
  549.0 10.0 slice-start.1
  559.0 56.0 %copy-start.38 = (f32[1536]{0:T(1024)S(1)}, f32[1536]{0:T(1024)}, u32[]{:S(2)}) copy-start(f32[1536]{0:T(1024)} %copy-done.37) | copy-start | bytes 18436
  562.3 59.0 %copy-start.30 = (f32[3,576]{1,0:T(4,128)S(1)}, f32[3,576]{1,0:T(4,128)}, u32[]{:S(2)}) copy-start(f32[3,576]{1,0:T(4,128)} %copy-done.29) | copy-start | bytes 20740
  562.3 59.0 %copy-start.32 = (f32[3,576]{1,0:T(4,128)S(1)}, f32[3,576]{1,0:T(4,128)}, u32[]{:S(2)}) copy-start(f32[3,576]{1,0:T(4,128)} %copy-done.31) | copy-start | bytes 20740
  (42 other events, 197.2 us)
Sparse Core Ops, SparseCore 0:
  87.8 112.0 all-reduce.7
  231.7 112.9 all-reduce.11
  424.7 112.9 all-reduce.13
  540.9 74.0 all-reduce.9
  625.3 407.6 all-reduce.15
where the time goes:
time: 1060 us; the launch traced here: 1050 us
  waiting for transfers between devices  707 us (67%)
  matrix products  183 us (17%)
  other arithmetic  65.1 us (6%)
  local copies, waits for them, and re-layouts  37.5 us (4%)
  blocking collectives  29.3 us (3%)
  between operations  15.1 us (1%)
  loops' own time  12.1 us (1%)
    psum x1, waiting for transfers between devices, local(): lax.psum((ada_grad, ada_bias_grad, qkv_grad, qv_bias_grad, proj_grad, pro...  363 us
    psum x1, waiting for transfers between devices, local(): grad_h_two = lax.psum(h_two_part, 'head')  113 us
    psum x1, waiting for transfers between devices, local(): branch_a = lax.psum(attn_part, 'head') + proj_b  92.8 us
    psum x1, waiting for transfers between devices, local(): grad_h_one = lax.psum(h_one_part, 'head')  85.4 us
    psum x1, waiting for transfers between devices, local(): lax.psum(mlp_part.astype(jnp.bfloat16), 'head').astype(jnp.float32) + fc2_b  52.6 us
    dot_general x7, matrix products, per_token(): return jnp.dot(select, table, precision=highest)  39.1 us
    dot_general x6, matrix products, item_sums(): return jnp.einsum('sg,sd->gd', select, values, precision=highest)  30.8 us
  transfers between devices with their start and end apart: 5, of which 5 were waited for; matrix products, arithmetic and copies ran while one was open for 9% of the time, Pallas kernels for 0%

commit v1 on v0

--- a/solution.py
+++ b/solution.py
@@ -163,8 +163,8 @@
         jnp.float32
     )
     modulation = lax.all_gather(mod_part, "head", axis=1, tiled=True)
-    shift_one, scale_one, gate_one, shift_two, scale_two, gate_two = [
-        per_token(select, table_piece) for table_piece in jnp.split(modulation, 6, axis=1)
+    shift_one, scale_one = [
+        per_token(select, modulation[:, k * model_width : (k + 1) * model_width]) for k in (0, 1)
     ]
     x_full = tokens.astype(jnp.float32)
     norm_one = normalize(x_full)
@@ -179,38 +179,53 @@
     )
     head_keep = jnp.repeat(per_token(select, head_masks.astype(jnp.float32)), HEAD_DIM, axis=1)
     attn_low = (attended * head_keep).astype(jnp.bfloat16)
-    attn_part = jnp.dot(attn_low, proj_weight, preferred_element_type=jnp.float32)
     proj_b = proj_bias.astype(jnp.float32)
     fc1_b = fc1_bias.astype(jnp.float32)
     fc2_b = fc2_bias.astype(jnp.float32)
-    branch_a = lax.psum(attn_part, "head") + proj_b
-    mid_rows = x_full + gate_one * branch_a
+
+    def scatter_sum(part):
+        return lax.psum_scatter(
+            part.astype(jnp.bfloat16), "head", scatter_dimension=0, tiled=True
+        ).astype(jnp.float32)
+
+    def share_rows_of(value):
+        return lax.all_gather(value, "head", axis=0, tiled=True)
+
+    attn_part = jnp.dot(attn_low, proj_weight, preferred_element_type=jnp.float32)
+    branch_a = scatter_sum(attn_part) + proj_b
+    x_own = own_rows(tokens).astype(jnp.float32)
+    select_own = own_rows(select)
+    keep_own = own_rows(keep_tok)
+    cot_own = own_rows(out_cotangent).astype(jnp.float32)
+    shift_one_o, scale_one_o, gate_one_o, shift_two_o, scale_two_o, gate_two_o = jnp.split(
+        per_token(select_own, modulation), 6, axis=1
+    )
+    mid_rows = x_own + gate_one_o * branch_a
     norm_two = normalize(mid_rows)
-    h_two = (norm_two * (1.0 + scale_two) + shift_two).astype(jnp.bfloat16)
+    h_two = share_rows_of((norm_two * (1.0 + scale_two_o) + shift_two_o).astype(jnp.bfloat16))
     hidden = jnp.dot(h_two, fc1_weight, preferred_element_type=jnp.float32) + fc1_b
     gelu_out = gelu_tanh(hidden).astype(jnp.bfloat16)
     mlp_part = jnp.dot(gelu_out, fc2_weight, preferred_element_type=jnp.float32)
-    grad_y = out_cotangent.astype(jnp.float32)
-    grad_m = (grad_y * gate_two * keep_tok).astype(jnp.bfloat16)
-    branch_m = lax.psum(mlp_part.astype(jnp.bfloat16), "head").astype(jnp.float32) + fc2_b
-    layer_full = mid_rows + gate_two * keep_tok * branch_m
-    layer_out = own_rows(layer_full).astype(jnp.bfloat16)
-    gate_two_grad = item_sums(select, grad_y * keep_tok * branch_m)
+    gate_two = per_token(select, modulation[:, 5 * model_width :])
+    grad_m = (out_cotangent.astype(jnp.float32) * gate_two * keep_tok).astype(jnp.bfloat16)
+    grad_gelu = jnp.einsum("sd,fd->sf", grad_m, fc2_weight, preferred_element_type=jnp.float32)
+    grad_hidden = jax.vjp(gelu_tanh, hidden)[1](grad_gelu)[0].astype(jnp.bfloat16)
+    h_two_part = jnp.einsum(
+        "sf,df->sd", grad_hidden, fc1_weight, preferred_element_type=jnp.float32
+    )
+    grad_h_two = scatter_sum(h_two_part)
     fc2_grad = jnp.einsum("sf,sd->fd", gelu_out, grad_m, preferred_element_type=jnp.float32)
     fc2_bias_grad = jnp.sum(grad_m.astype(jnp.float32), axis=0)
-    grad_gelu = jnp.einsum("sd,fd->sf", grad_m, fc2_weight, preferred_element_type=jnp.float32)
-    grad_hidden = jax.vjp(gelu_tanh, hidden)[1](grad_gelu)[0].astype(jnp.bfloat16)
     fc1_grad = jnp.einsum("sd,sf->df", h_two, grad_hidden, preferred_element_type=jnp.float32)
     fc1_bias_grad = jnp.sum(grad_hidden.astype(jnp.float32), axis=0)
-    h_two_part = jnp.einsum(
-        "sf,df->sd", grad_hidden, fc1_weight, preferred_element_type=jnp.float32
-    )
-    grad_h_two = lax.psum(h_two_part, "head")
-    grad_mid = grad_y + norm_back(mid_rows, grad_h_two * (1.0 + scale_two))
-    shift_two_grad = item_sums(select, grad_h_two)
-    scale_two_grad = item_sums(select, grad_h_two * norm_two)
-    gate_one_grad = item_sums(select, grad_mid * branch_a)
-    grad_a = (grad_mid * gate_one).astype(jnp.bfloat16)
+    branch_m = scatter_sum(mlp_part) + fc2_b
+    layer_out = (mid_rows + gate_two_o * keep_own * branch_m).astype(jnp.bfloat16)
+    gate_two_grad = item_sums(select_own, cot_own * keep_own * branch_m)
+    grad_mid = cot_own + norm_back(mid_rows, grad_h_two * (1.0 + scale_two_o))
+    shift_two_grad = item_sums(select_own, grad_h_two)
+    scale_two_grad = item_sums(select_own, grad_h_two * norm_two)
+    gate_one_grad = item_sums(select_own, grad_mid * branch_a)
+    grad_a = share_rows_of((grad_mid * gate_one_o).astype(jnp.bfloat16))
     proj_bias_grad = jnp.sum(grad_a.astype(jnp.float32), axis=0)
     proj_grad = jnp.einsum("sj,sd->jd", attn_low, grad_a, preferred_element_type=jnp.float32)
     grad_attn_low = jnp.einsum(
@@ -239,11 +254,10 @@
     h_one_part = jnp.einsum(
         "csj,dcj->sd", grad_three, qkv_weight, preferred_element_type=jnp.float32
     )
-    grad_h_one = lax.psum(h_one_part, "head")
-    grad_input = grad_mid + norm_back(x_full, grad_h_one * (1.0 + scale_one))
-    input_grad = own_rows(grad_input)
-    shift_one_grad = item_sums(select, grad_h_one)
-    scale_one_grad = item_sums(select, grad_h_one * norm_one)
+    grad_h_one = scatter_sum(h_one_part)
+    input_grad = grad_mid + norm_back(x_own, grad_h_one * (1.0 + scale_one_o))
+    shift_one_grad = item_sums(select_own, grad_h_one)
+    scale_one_grad = item_sums(select_own, grad_h_one * normalize(x_own))
     mod_grad = jnp.concatenate(
         [
             shift_one_grad,
@@ -255,26 +269,38 @@
         ],
         axis=1,
     )
-    col_count = ada_weight.shape[1]
-    mod_cols = lax.dynamic_slice_in_dim(mod_grad, lax.axis_index("head") * col_count, col_count, 1)
-    ada_grad = jnp.einsum("gd,gc->dc", time_act.astype(jnp.float32), mod_cols, precision=highest)
-    ada_bias_grad = jnp.sum(mod_cols, axis=0)
+    mod_cols = lax.psum_scatter(mod_grad, "head", scatter_dimension=1, tiled=True)
+    all_cols = lax.all_gather(mod_cols, "dp", axis=0, tiled=True)
+    all_act = lax.all_gather(time_act, "dp", axis=0, tiled=True)
+    ada_grad = jnp.einsum("gd,gc->dc", all_act.astype(jnp.float32), all_cols, precision=highest)
+    ada_bias_grad = jnp.sum(all_cols, axis=0)
     summed = lax.psum(
         (
-            ada_grad,
-            ada_bias_grad,
-            qkv_grad,
-            qv_bias_grad,
-            proj_grad,
-            proj_bias_grad,
-            fc1_grad,
-            fc1_bias_grad,
-            fc2_grad,
-            fc2_bias_grad,
+            qkv_grad.astype(jnp.bfloat16),
+            proj_grad.astype(jnp.bfloat16),
+            fc1_grad.astype(jnp.bfloat16),
+            fc2_grad.astype(jnp.bfloat16),
         ),
         "dp",
     )
-    return (layer_out, input_grad) + tuple(summed)
+    qkv_grad, proj_grad, fc1_grad, fc2_grad = [g.astype(jnp.float32) for g in summed]
+    qv_bias_grad, proj_bias_grad, fc1_bias_grad, fc2_bias_grad = lax.psum(
+        (qv_bias_grad, proj_bias_grad, fc1_bias_grad, fc2_bias_grad), "dp"
+    )
+    return (
+        layer_out,
+        input_grad,
+        ada_grad,
+        ada_bias_grad,
+        qkv_grad,
+        qv_bias_grad,
+        proj_grad,
+        proj_bias_grad,
+        fc1_grad,
+        fc1_bias_grad,
+        fc2_grad,
+        fc2_bias_grad,
+    )
 
 
 def solution(mesh):

time: 1060 us -> 684 us (0.65)
  waiting for transfers between devices: 707 us -> 380 us
  matrix products: 183 us -> 135 us
  blocking collectives: 29.3 us -> 48.6 us
  other arithmetic: 65.1 us -> 51.5 us
    psum x5 -> x1, waiting for transfers between devices: 707 us -> 112 us  [local(): lax.psum((qkv_grad.astype(jnp.bfloat16), proj_grad.astype(jnp.bfloat16),...]
    reduce_scatter x0 -> x4, waiting for transfers between devices: none -> 177 us  [scatter_sum(): lax.psum_scatter(part.astype(jnp.bfloat16), 'head', scatter_dimension=0,...]
    all_gather x0 -> x2, waiting for transfers between devices: none -> 46.2 us  [share_rows_of(): return lax.all_gather(value, 'head', axis=0, tiled=True)]
    unnamed x5 -> x9, waiting for transfers between devices: 0.08 us -> 45.7 us
    dot_general x6, matrix products: 30.8 us -> 6.08 us  [item_sums(): return jnp.einsum('sg,sd->gd', select, values, precision=highest)]
    all_gather x0 -> x2, blocking collectives: none -> 22.4 us  [the longest x1 12.1 us: local(): all_act = lax.all_gather(time_act, 'dp', axis=0, tiled=True)]
    dot_general x7 -> x5, matrix products: 39.1 us -> 20.8 us  [per_token(): return jnp.dot(select, table, precision=highest)]
    reduce_sum x2 -> x1, other arithmetic: 16.4 us -> 1.54 us  [normalize(): center * lax.rsqrt(jnp.mean(center * center, axis=-1, keepdims=True) + 1e...]
  transfers between devices with their start and end apart: 5 -> 8, of which waited for: 5 -> 8; matrix products, arithmetic and copies ran while one was open for 9% -> 8% of each run, Pallas kernels for 0% -> 0%
where the time goes in v1:
time: 684 us; the launch traced here: 675 us
  waiting for transfers between devices  380 us (56%)
  matrix products  135 us (20%)
  other arithmetic  51.5 us (8%)
  blocking collectives  48.6 us (7%)
  local copies, waits for them, and re-layouts  32.6 us (5%)
  between operations  14.9 us (2%)
  loops' own time  12.6 us (2%)
    reduce_scatter x4, waiting for transfers between devices, scatter_sum(): lax.psum_scatter(part.astype(jnp.bfloat16), 'head', scatter_dimension=0,...  177 us
    psum x1, waiting for transfers between devices, local(): lax.psum((qkv_grad.astype(jnp.bfloat16), proj_grad.astype(jnp.bfloat16),...  112 us
    all_gather x2, waiting for transfers between devices, share_rows_of(): return lax.all_gather(value, 'head', axis=0, tiled=True)  46.2 us
    unnamed x9, waiting for transfers between devices  45.7 us
    dot_general x5, matrix products, per_token(): return jnp.dot(select, table, precision=highest)  20.8 us
    dot_general x6, matrix products, one_block(): jnp.einsum('qhe,khe->hqk', q_block, k_heads, preferred_element_type=jnp.f...  17.9 us
    psum x1, blocking collectives, local(): lax.psum((qv_bias_grad, proj_bias_grad, fc1_bias_grad, fc2_bias_grad), 'dp')  16 us
  transfers between devices with their start and end apart: 8, of which 8 were waited for; matrix products, arithmetic and copies ran while one was open for 8% of the time, Pallas kernels for 0%

profile of v1, /device:TPU:29, one launch (start us, length us, event | category | flops | bytes accessed | tf_op | source)
XLA Modules:
  0.0 675.5 jit_solution(17424533891599629888)
XLA Ops:
  14.4 10.3 %all-gather = f32[8,864,3]{1,2,0:T(4,128)S(1)} all-gather(f32[1,864,3]{1,2,0:T(4,128)S(1)} %fusion.47), channel_id=1, replica_groups=mesh['dp'=4,'head'=8] {'head'}, dimensions={0}, use_global_device_ids=true | all-gather | bytes 93312 | tf_op jit(solution)/shard_map/all_gather | solution.py:165
  24.8 6.0 fusion.28
  39.5 43.2 %while.27 = (s32[]{:T(128)}, f32[3,512,144]{1,0,2:T(4,128)S(1)}, f32[3,2,512]{2,1,0:T(2,128)S(1)}, s32[3]{0:T(128)S(1)}, s32[1536]{0:T(1024)S(1)}, /*index=5*/s3...) while((s32[]{:T(128)}, f32[3,512,144]{1,0,2:T(4,128)S(1)}, ...), condition=%wide.region_5.6_spmd, body=%wide.region_2.5_spmd.sunk | while | flops 472644608 | bytes 24584384 | solution.py:66
  87.1 4.5 fusion.84
  91.6 42.8 %reduce-scatter.8.cloned.1.call-done = bf16[192,1152]{1,0:T(8,128)(2,1)} async-done(((bf16[1536,1152]{1,0:T(8,128)(2,1)}), bf16[192,1152]{1,0:T(8,128)(2,1)}) %reduce-scatter.8.cloned.1.call-update) | async-done | bytes 442384 | tf_op jit(solution)/shard_map/reduce_scatter | solution.py:187
  139.1 6.0 convert_reduce_fusion.1
  146.8 4.3 fusion.91
  151.1 22.3 %all-gather.6.cloned.1.call-done = bf16[1536,1152]{1,0:T(8,128)(2,1)} async-done(((bf16[192,1152]{1,0:T(8,128)(2,1)}), bf16[1536,1152]{1,0:T(8,128)(2,1)}) %all-gather.6.cloned.1.call-update) | async-done | bytes 3538960 | tf_op jit(solution)/shard_map/all_gather | solution.py:192
  173.4 8.7 %convert_reduce_fusion.3 = (f32[576]{0:T(1024)S(1)}, bf16[1536,576]{0,1:T(8,128)(2,1)S(1)}, f32[1536,576]{0,1:T(8,128)}) fusion(f32[1536,576]{0,1:T(8,128)} %fusion.91, f32[576]{0:T(1024)S(1)} %convert_element_type.194, bf16[1536,1152]{1,0:T(8,128)(2,1)} %all-gather.6.cloned.1.call-done, bf16[1152,576]{0,1:T(8,128)(2,1)S(1)} %copy-done.33), kind=kOutput, calls=%fused_computation.64 | convolution fusion | flops 2058780160 | bytes 13718016 | tf_op jit(solution)/shard_map/dot_general | solution.py:206
  183.2 4.6 convolution_convert_fusion.1
  189.2 7.3 %convolution_convert_fusion.2 = bf16[1536,1152]{1,0:T(8,128)(2,1)} fusion(bf16[576,1152]{1,0:T(8,128)(2,1)S(1)} %copy-done.35, f32[1536,576]{0,1:T(8,128)} %get-tuple-element.244), kind=kOutput, calls=%fused_computation.50 | convolution fusion | flops 2048163840 | bytes 8404992 | tf_op jit(solution)/shard_map/dot_general | solution.py:208
  197.3 38.6 %reduce-scatter.12.cloned.1.call-done = bf16[192,1152]{1,0:T(8,128)(2,1)} async-done(((bf16[1536,1152]{1,0:T(8,128)(2,1)}), bf16[192,1152]{1,0:T(8,128)(2,1)}) %reduce-scatter.12.cloned.1.call-update) | async-done | bytes 442384 | tf_op jit(solution)/shard_map/reduce_scatter | solution.py:187
  237.4 49.9 %reduce-scatter.10.cloned.1.call-done = bf16[192,1152]{1,0:T(8,128)(2,1)} async-done(((bf16[1536,1152]{1,0:T(8,128)(2,1)}), bf16[192,1152]{1,0:T(8,128)(2,1)}) %reduce-scatter.10.cloned.1.call-update) | async-done | bytes 442384 | tf_op jit(solution)/shard_map/reduce_scatter | solution.py:187
  293.0 6.2 convolution_convert_fusion.3
  299.2 4.2 convolution_convert_fusion.4
  303.3 23.9 %all-gather.8.cloned.1.call-done = bf16[1536,1152]{1,0:T(8,128)(2,1)} async-done(((bf16[192,1152]{1,0:T(8,128)(2,1)}), bf16[1536,1152]{1,0:T(8,128)(2,1)}) %all-gather.8.cloned.1.call-update) | async-done | bytes 3538960 | tf_op jit(solution)/shard_map/all_gather | solution.py:192
  327.3 4.1 fusion.42
  331.3 48.1 %while.28 = (s32[]{:T(128)}, f32[1536,2,72]{0,2,1:T(8,128)}, f32[1536,2,72]{0,2,1:T(8,128)S(1)}, bf16[3,512,144]{1,2,0:T(8,128)(2,1)}, s32[3]{0:T(128)S(1)}, /*i...) while((s32[]{:T(128)}, f32[1536,2,72]{0,2,1:T(8,128)}, ...), condition=%wide.region_15.16_spmd.clone, body=%wide.region_13.15_spmd.clone.sunk | while | flops 1148435456 | bytes 61780260 | solution.py:121
  395.2 12.1 %all-gather.1 = bf16[4,3,1152]{2,1,0:T(4,128)(2,1)S(1)} all-gather(bf16[1,3,1152]{2,1,0:T(4,128)(2,1)S(1)} %fusion.129), channel_id=1, replica_groups=mesh['dp'=4,'head'=8] {'dp'}, dimensions={0}, use_global_device_ids=true | all-gather | bytes 34560 | tf_op jit(solution)/shard_map/all_gather | solution.py:274
  410.2 16.0 %all-reduce = (f32[2,144]{1,0:T(2,128)}, f32[1152]{0:T(1024)}, f32[576]{0:T(1024)}, f32[1152]{0:T(1024)}) all-reduce(f32[2,144]{1,0:T(2,128)S(1)} %pad_maximum_fusion.2, f32[1152]{0:T(1024)S(1)} %convert_reduce_fusion.2, f32[576]{0:T(1024)S(1)} %get-tuple-element.222, ...), channel_id=1, replica_groups=mesh['dp'=4,'head'=8] {'dp'}, use_global_device_ids=true, to_apply=%region_26.27 | all-reduce | flops 3168 | bytes 25344 | tf_op jit(solution)/shard_map/psum | solution.py:287
  426.2 111.7 %all-reduce.4.cloned.1.call-done = (bf16[1152,3,144]{0,2,1:T(8,128)(2,1)}, bf16[144,1152]{1,0:T(8,128)(2,1)}, bf16[1152,576]{0,1:T(8,128)(2,1)}, bf16[576,1152]{1,0:T(8,128)(2,1)}) async-done(((bf16[1152,3,144]{0,2,1:T(8,128)(2,1)}, bf16[144,1152]{1,0:T(8,128)(2,1)}, bf16[1152,576]{0,1:T(8,128)(2,1)}, bf16[576,1152]{1,0:T(8,128)(2,1)}), (bf16[1152,3,144]{0,2,1:T(8,128)(2,1)}, bf16[144,1152]{1,0:T(8,128)(2,1)}, ...) | async-done | bytes 3981328 | tf_op jit(solution)/shard_map/psum | solution.py:277
  546.0 45.3 %reduce-scatter.14.cloned.1.call-done = bf16[192,1152]{1,0:T(8,128)(2,1)} async-done(((bf16[1536,1152]{1,0:T(8,128)(2,1)}), bf16[192,1152]{1,0:T(8,128)(2,1)}) %reduce-scatter.14.cloned.1.call-update) | async-done | bytes 442384 | tf_op jit(solution)/shard_map/reduce_scatter | solution.py:187
  607.1 45.6 %reduce-scatter.16.cloned.1.call-done = f32[864,3]{1,0:T(8,128)} async-done(((f32[6912,3]{1,0:T(8,128)}), f32[864,3]{1,0:T(8,128)}) %reduce-scatter.16.cloned.1.call-update) | async-done | bytes 10384
  653.8 10.3 %all-gather.2 = f32[4,3,864]{2,1,0:T(4,128)S(1)} all-gather(f32[1,3,864]{2,1,0:T(4,128)S(1)} %bitcast.149), channel_id=1, replica_groups=mesh['dp'=4,'head'=8] {'dp'}, dimensions={0}, use_global_device_ids=true | all-gather | bytes 51840 | tf_op jit(solution)/shard_map/all_gather | solution.py:273
  (261 shorter events, 163.5 us)
Async XLA Ops:
  7.2 6.6 copy-start
  7.2 127.2 %reduce-scatter.8.cloned.1.call-start = ((), (), s32[]{:S(2)}) async-start(), calls=%async_computation.5 | async-start | bytes 3981312 | tf_op jit(solution)/shard_map/reduce_scatter | solution.py:187
  13.8 17.1 %copy-start.24 = (f32[3,576]{1,0:T(4,128)}, f32[3,576]{1,0:T(4,128)S(1)}, u32[]{:S(2)}) copy-start(f32[3,576]{1,0:T(4,128)S(1)} %get-tuple-element.240) | copy-start | bytes 20740
  13.8 17.1 %copy-start.26 = (f32[3,576]{1,0:T(4,128)}, f32[3,576]{1,0:T(4,128)S(1)}, u32[]{:S(2)}) copy-start(f32[3,576]{1,0:T(4,128)S(1)} %get-tuple-element.241) | copy-start | bytes 20740
  86.7 86.6 %all-gather.6.cloned.1.call-start = ((), (), s32[]{:S(2)}) async-start(), calls=%async_computation.6 | async-start | bytes 3981312 | tf_op jit(solution)/shard_map/all_gather | solution.py:192
  91.6 47.4 %copy-start.31 = (bf16[576]{0:T(1024)(128)(2,1)S(1)}, bf16[576]{0:T(1024)(128)(2,1)}, u32[]{:S(2)}) copy-start(bf16[576]{0:T(1024)(128)(2,1)} %param.32) | copy-start | bytes 3460
  91.6 47.4 %copy-start.28 = (s32[1,1536]{1,0:T(1,128)S(1)}, s32[1,1536]{1,0:T(1,128)}, u32[]{:S(2)}) copy-start(s32[1,1536]{1,0:T(1,128)} %param.24) | copy-start | bytes 18436
  138.9 96.9 %reduce-scatter.12.cloned.1.call-start = ((), (), s32[]{:S(2)}) async-start(), calls=%async_computation.8 | async-start | bytes 3981312 | tf_op jit(solution)/shard_map/reduce_scatter | solution.py:187
  139.0 7.8 %copy-start.34 = (bf16[576,1152]{1,0:T(8,128)(2,1)S(1)}, bf16[576,1152]{1,0:T(8,128)(2,1)}, u32[]{:S(2)}) copy-start(bf16[576,1152]{1,0:T(8,128)(2,1)} %param.33) | copy-start | bytes 3981316
  146.8 26.6 %copy-start.33 = (bf16[1152,576]{0,1:T(8,128)(2,1)S(1)}, bf16[1152,576]{0,1:T(8,128)(2,1)}, u32[]{:S(2)}) copy-start(bf16[1152,576]{0,1:T(8,128)(2,1)} %param.31) | copy-start | bytes 3981316
  187.9 99.4 %reduce-scatter.10.cloned.1.call-start = ((), (), s32[]{:S(2)}) async-start(), calls=%async_computation.7 | async-start | bytes 3981312 | tf_op jit(solution)/shard_map/reduce_scatter | solution.py:187
  196.5 130.7 %all-gather.8.cloned.1.call-start = ((), (), s32[]{:S(2)}) async-start(), calls=%async_computation.9 | async-start | bytes 3981312 | tf_op jit(solution)/shard_map/all_gather | solution.py:192
  292.8 245.1 %all-reduce.4.cloned.1.call-start = ((), (), s32[]{:S(2)}) async-start(), calls=%async_computation.12 | async-start | bytes 7962624 | tf_op jit(solution)/shard_map/psum | solution.py:277
  292.9 6.2 copy-start.40
  299.2 28.1 %copy-start.23 = (bf16[144,1152]{1,0:T(8,128)(2,1)S(1)}, bf16[144,1152]{1,0:T(8,128)(2,1)}, u32[]{:S(2)}) copy-start(bf16[144,1152]{1,0:T(8,128)(2,1)} %param.29) | copy-start | bytes 995332
  389.1 202.2 %reduce-scatter.14.cloned.1.call-start = ((), (), s32[]{:S(2)}) async-start(), calls=%async_computation.10 | async-start | bytes 3981312 | tf_op jit(solution)/shard_map/reduce_scatter | solution.py:187
  394.4 13.1 %copy-start.15 = (bf16[3,512,144]{1,2,0:T(8,128)(2,1)S(1)}, bf16[3,512,144]{1,2,0:T(8,128)(2,1)}, u32[]{:S(2)}) copy-start(bf16[3,512,144]{1,2,0:T(8,128)(2,1)} %get-tuple-element.126) | copy-start | bytes 1327108
  394.4 258.3 %reduce-scatter.16.cloned.1.call-start = ((), (), s32[]{:S(2)}) async-start(), calls=%async_computation.11 | async-start | bytes 3981312
  544.3 51.7 %copy-start.20 = (pred[1536,3]{1,0:T(32,128)(4,1)S(1)}, pred[1536,3]{1,0:T(32,128)(4,1)}, u32[]{:S(2)}) copy-start(pred[1536,3]{1,0:T(32,128)(4,1)} %copy-done.19) | copy-start | bytes 13828
  546.0 51.9 %copy-start.7 = (f32[192,1152]{1,0:T(8,128)S(1)}, f32[192,1152]{1,0:T(8,128)}, u32[]{:S(2)}) copy-start(f32[192,1152]{1,0:T(8,128)} %copy-done.6) | copy-start | bytes 2654212
  546.0 51.9 %copy-start.14 = (bf16[192,1152]{1,0:T(8,128)(2,1)S(1)}, bf16[192,1152]{1,0:T(8,128)(2,1)}, u32[]{:S(2)}) copy-start(bf16[192,1152]{1,0:T(8,128)(2,1)} %reduce-scatter.8.cloned.1.call-done) | copy-start | bytes 1327108
  546.0 53.6 %copy-start.8 = (bf16[192,1152]{1,0:T(8,128)(2,1)S(1)}, bf16[192,1152]{1,0:T(8,128)(2,1)}, u32[]{:S(2)}) copy-start(bf16[192,1152]{1,0:T(8,128)(2,1)} %reduce-scatter.12.cloned.1.call-done) | copy-start | bytes 1327108
  593.2 7.2 %copy-start.21 = (bf16[192,1152]{1,0:T(8,128)(2,1)S(1)}, bf16[192,1152]{1,0:T(8,128)(2,1)}, u32[]{:S(2)}) copy-start(bf16[192,1152]{1,0:T(8,128)(2,1)} %reduce-scatter.10.cloned.1.call-done) | copy-start | bytes 1327108
  604.4 64.0 %copy-start.1 = (bf16[1152,864]{0,1:T(8,128)(2,1)S(1)}, bf16[1152,864]{0,1:T(8,128)(2,1)}, u32[]{:S(2)}) copy-start(bf16[1152,864]{0,1:T(8,128)(2,1)} %param.25) | copy-start | bytes 5971972
  (31 other events, 73.1 us)
Sparse Core Ops, SparseCore 0:
  86.8 47.5 reduce-scatter.7
  139.0 34.2 all-gather.5
  188.0 47.7 reduce-scatter.11
  239.2 48.0 reduce-scatter.9
  292.9 34.2 all-gather.7
  389.3 148.5 all-reduce.3
  542.3 48.9 reduce-scatter.13
  604.6 48.0 reduce-scatter.15
